TPU v7x, 32 devices: a whole 2x2x4 slice. The times are simulated.
32 devices in a mesh: group: 2 (over y), phi: 4 (over z), eta: 2 (over x), half: 2 (over core).
Axes of the slice: x: 2, y: 2, z: 4, core: 2. Of those that a mesh axis runs over, the one named last changes fastest.
Arguments:
- feats: bfloat16 [8, 2, 512, 512], P(('group', 'phi'), 'eta', 'half'), parts along dimension 0, may hold values from -6 to 6
- cotangent: bfloat16 [8, 2, 512, 512], P(('group', 'phi'), 'eta', 'half'), parts along dimension 0, may hold values from -6 to 6
- tiles: bfloat16 [8, 2, 24, 128, 128], P(('group', 'phi'), 'eta', 'half'), parts along dimension 0, may hold values from -0.21875 to 0.21875
- tile_src: int32 [8, 2, 24], P(('group', 'phi'), 'eta', 'half'), parts along dimension 0, may hold values from 0 to 5
- tile_dst: int32 [8, 2, 24], P(('group', 'phi'), 'eta', 'half'), parts along dimension 0, may hold values from -1 to 3, as said below
- weights: bfloat16 [2, 512, 512], replicated, may hold values from -0.25 to 0.25
- mask: int32 [2, 8, 8], replicated, may hold values 0 or 1
- counts: int32 [8, 2], P(('group', 'phi'), 'eta'), parts along dimension 0, may hold values from 128 to 512, as said below
Outputs:
- final: bfloat16 [8, 2, 512, 512], P(('group', 'phi'), 'eta', 'half'), parts along dimension 0
- grad_w: float32 [4, 512, 512], P('group', 'phi'), parts along dimension 0
There are 2 independent parts, one for each index of `group`. A program takes and returns all parts, laid end to end along the dimension named above; an argument that names none is the same for every part. Nothing has to cross between parts.
Inputs may be any that keep to these rules, and one draw needn't show every extreme that they name: `tile_dst`: in each region half the live tiles fill the first slots and the rest hold -1; some region half has all 12 slots live. `counts`: some region is full and some holds a quarter of its hits.
All inputs are finite; a program needn't handle non-finite values.
Results may differ from a plain program's by a relative error of at most 0.017.
Values may be sent and summed in bfloat16 or wider, within the bound.
No kernel may reach another device: no remote copies, remote signals or barrier semaphores. Data moves between devices by JAX's collectives and lax.ppermute only.
A program may use at most 64 MiB of HBM per device.

v0:
```python
import jax
import jax.numpy as jnp
from jax import lax
from jax.sharding import PartitionSpec as P


def with_halo(block, sides, width, periodic):
    for axis, dim in sides:
        count = lax.axis_size(axis)
        forward = [(i, i + 1) for i in range(count - 1)]
        if periodic:
            forward.append((count - 1, 0))
        backward = [(target, source) for source, target in forward]
        low = lax.ppermute(
            lax.slice_in_dim(block, block.shape[dim] - width, None, axis=dim), axis, forward
        )
        high = lax.ppermute(lax.slice_in_dim(block, 0, width, axis=dim), axis, backward)
        block = jnp.concatenate([low, block, high], axis=dim)
    return block


def silu_slope(pre):
    sigma = jax.nn.sigmoid(pre)
    return sigma * (1.0 + pre * (1.0 - sigma))


def body(feats, cotangent, tiles, tile_src, tile_dst, weights, mask, counts):
    rows = feats.shape[2]
    width = feats.shape[3]
    block = tiles.shape[3]
    own_blocks = rows // block
    halves = lax.axis_size("half")
    region_blocks = own_blocks * halves
    slots = own_blocks + 4
    layers = weights.shape[0]
    grid = mask.shape[1]
    side = width // grid
    tile_set = tiles[0, 0]
    sources_of = tile_src[0, 0]
    targets = tile_dst[0, 0]
    first_row = lax.axis_index("half") * rows
    live = (first_row + jnp.arange(rows, dtype=jnp.int32) < counts[0, 0]).astype(jnp.float32)[
        :, None
    ]
    eta_here = lax.axis_index("eta")
    lower_eta = (eta_here > 0).astype(jnp.bfloat16)
    upper_eta = (eta_here < lax.axis_size("eta") - 1).astype(jnp.bfloat16)
    mask_full = (
        jnp.broadcast_to(mask[:, :, None, :, None], (layers, grid, side, grid, side))
        .reshape(layers, width, width)
        .astype(jnp.float32)
    )
    masked = (weights.astype(jnp.float32) * mask_full).astype(jnp.bfloat16)
    block_ids = jnp.arange(region_blocks, dtype=jnp.int32)
    slot_ids = jnp.arange(slots, dtype=jnp.int32)
    state = feats[0, 0]
    inputs = []
    pres = []
    for layer in range(layers):
        edge = state[:block][None, None]
        padded = with_halo(edge, (("phi", 0), ("eta", 1)), 1, True)
        rims = jnp.stack(
            [padded[0, 1], padded[2, 1], padded[1, 0] * lower_eta, padded[1, 2] * upper_eta]
        )
        messages_picked = jnp.take(
            jnp.concatenate([state.reshape(own_blocks, block, width), rims], axis=0),
            sources_of,
            axis=0,
        )
        messages_parts = jnp.einsum(
            "tij,tjd->tid", tile_set, messages_picked, preferred_element_type=jnp.float32
        )
        messages_onehot = (targets[None, :] == block_ids[:, None]).astype(jnp.float32)
        messages_total = jnp.einsum(
            "bt,tid->bid", messages_onehot, messages_parts, precision=lax.Precision.HIGHEST
        )
        region = messages_total.reshape(region_blocks * block, width)
        gathered = lax.psum_scatter(
            region.astype(jnp.bfloat16), "half", scatter_dimension=0, tiled=True
        ).astype(jnp.float32)
        hfloat = state.astype(jnp.float32)
        mixed = (hfloat + gathered).astype(jnp.bfloat16)
        pre = jnp.dot(mixed, masked[layer], preferred_element_type=jnp.float32)
        state = (live * (hfloat + jax.nn.silu(pre))).astype(jnp.bfloat16)
        inputs.append(mixed)
        pres.append(pre)
    upstream = cotangent[0, 0].astype(jnp.float32)
    partials = [None] * layers
    for layer in reversed(range(layers)):
        delta = (upstream * live * silu_slope(pres[layer])).astype(jnp.bfloat16)
        partials[layer] = (
            jnp.einsum("rd,re->de", inputs[layer], delta, preferred_element_type=jnp.float32)
            * mask_full[layer]
        )
        if layer > 0:
            back = jnp.einsum(
                "re,de->rd", delta, masked[layer], preferred_element_type=jnp.float32
            ).astype(jnp.bfloat16)
            whole = lax.all_gather(back, "half", axis=0, tiled=True)
            valid = (targets >= 0).astype(jnp.bfloat16)
            picked = (
                jnp.take(
                    whole.reshape(region_blocks, block, width), jnp.maximum(targets, 0), axis=0
                )
                * valid[:, None, None]
            )
            parts = jnp.einsum("tji,tjd->tid", tile_set, picked, preferred_element_type=jnp.float32)
            onehot = (sources_of[None, :] == slot_ids[:, None]).astype(jnp.float32)
            total = jnp.einsum("st,tid->sid", onehot, parts, precision=lax.Precision.HIGHEST)
            returned_phi = with_halo(
                total[own_blocks : own_blocks + 2].astype(jnp.bfloat16), (("phi", 0),), 1, True
            ).astype(jnp.float32)
            returned_eta = with_halo(
                total[own_blocks + 2 :].astype(jnp.bfloat16), (("eta", 0),), 1, False
            ).astype(jnp.float32)
            extra = returned_phi[0] + returned_phi[3] + returned_eta[0] + returned_eta[3]
            own = total[:own_blocks].reshape(rows, width)
            own = jnp.concatenate([own[:block] + extra, own[block:]], axis=0)
            upstream = live * upstream + back.astype(jnp.float32) + own
    stacked = jnp.stack(partials)
    shares = lax.psum_scatter(stacked.astype(jnp.bfloat16), "phi", scatter_dimension=1, tiled=True)
    result = lax.psum(shares, ("eta", "half")).astype(jnp.float32)
    return (state[None, None], result)


def solution(mesh):
    in_specs = (
        P(("group", "phi"), "eta", "half", None),
        P(("group", "phi"), "eta", "half", None),
        P(("group", "phi"), "eta", "half", None, None),
        P(("group", "phi"), "eta", "half"),
        P(("group", "phi"), "eta", "half"),
        P(),
        P(),
        P(("group", "phi"), "eta"),
    )
    out_specs = (P(("group", "phi"), "eta", "half", None), P("group", "phi", None))
    return jax.shard_map(body, mesh=mesh, in_specs=in_specs, out_specs=out_specs, check_vma=False)
```

profile of v0, /device:TPU:0, one launch (start us, length us, event | category | flops | bytes accessed | tf_op | source)
XLA Modules:
  0.0 213.0 jit_solution(10340029275667400948)
XLA Ops:
  8.2 3.1 %collective-permute-start = (bf16[1,1,128,512]{3,2,1,0:T(8,128)(2,1)S(1)}, bf16[1,1,128,512]{3,2,1,0:T(8,128)(2,1)S(1)}, u32[]{:S(2)}, u32[]{:S(2)}) collective-permute-start(bf16[1,1,128,512]{3,2,1,0:T(8,128)(2,1)S(1)} %slice.89), channel_id=1, source_target_pairs={{0,4},{4,8},{8,12},{12,0},{1,5},{5,9},{9,13},{13,1},{2,6},{6,10},{... | collective-permute-start | bytes 393224 | tf_op jit(solution)/shard_map/ppermute | solution.py:14
  21.2 10.0 %collective-permute-done.2 = bf16[3,1,128,512]{3,2,1,0:T(8,128)(2,1)S(1)} collective-permute-done((bf16[3,1,128,512]{3,2,1,0:T(8,128)(2,1)S(1)}, bf16[3,1,128,512]{3,2,1,0:T(8,128)(2,1)S(1)}, u32[]{:S(2)}, u32[]{:S(2)}) %collective-permute-start.2) | collective-permute-done | bytes 393248 | tf_op jit(solution)/shard_map/ppermute | solution.py:14
  31.2 6.8 %collective-permute-done.3 = bf16[3,1,128,512]{3,2,1,0:T(8,128)(2,1)S(1)} collective-permute-done((bf16[3,1,128,512]{3,2,1,0:T(8,128)(2,1)S(1)}, bf16[3,1,128,512]{3,2,1,0:T(8,128)(2,1)S(1)}, u32[]{:S(2)}, u32[]{:S(2)}) %collective-permute-start.3) | collective-permute-done | bytes 393248 | tf_op jit(solution)/shard_map/ppermute | solution.py:17
  42.0 3.5 %copy.19 = f32[12,512,128]{1,0,2:T(8,128)} copy(f32[12,512,128]{2,1,0:T(8,128)S(1)} %fusion.8) | data formatting | bytes 6291456 | tf_op jit(solution)/shard_map/tij,tjd->tid/dot_general | solution.py:70
  45.5 3.8 %fusion.16 = bf16[4,128,512]{2,0,1:T(4,128)(2,1)S(1)} fusion(f32[12,512,128]{1,0,2:T(8,128)} %copy.19, s32[12]{0:T(128)S(1)} %bitcast.122), kind=kOutput, calls=%fused_computation.22 | convolution fusion | flops 38010928 | bytes 3670064 | tf_op jit(solution)/shard_map/bt,tid->bid/dot_general | solution.py:74
  50.3 2.3 %broadcast_in_dim.41 = f32[2,8,64,8,64]{4,3,2,1,0:T(8,128)} broadcast(f32[2,8,8]{2,1,0:T(8,128)S(1)} %convert_element_type.115), dimensions={0,1,3} | broadcast | bytes 2097664 | tf_op jit(solution)/shard_map/broadcast_in_dim | solution.py:49
  52.6 3.5 %convert_element_type.116 = f32[2,512,512]{2,1,0:T(8,128)S(1)} reshape(f32[2,8,64,8,64]{4,3,2,1,0:T(8,128)} %broadcast_in_dim.41) | data formatting | bytes 4194304 | tf_op jit(solution)/shard_map/convert_element_type | solution.py:51
  58.7 2.4 %fusion.35 = (bf16[256,512]{1,0:T(8,128)(2,1)S(1)}, f32[256,512]{1,0:T(8,128)}) fusion(bf16[1,1,256,512]{3,2,1,0:T(8,128)(2,1)} %param.10, f32[256]{0:T(256)} %compare_convert_fusion.1, bf16[2,512,512]{2,1,0:T(8,128)(2,1)} %multiply_convert_fusion, bf16[256,512]{1,0:T(8,128)(2,1)} %reduce-scatter.4.cloned.1.call-done), kind=kOutput, calls=%fused_computation.43 | convolution fusion | flops 135790592 | bytes 2098176 | tf_op jit(solution)/shard_map/dot_general | solution.py:83
  65.0 4.4 %collective-permute-done.4 = bf16[1,1,128,512]{3,2,1,0:T(8,128)(2,1)S(1)} collective-permute-done((bf16[1,1,128,512]{3,2,1,0:T(8,128)(2,1)S(1)}, bf16[1,1,128,512]{3,2,1,0:T(8,128)(2,1)S(1)}, u32[]{:S(2)}, u32[]{:S(2)}) %collective-permute-start.4) | collective-permute-done | bytes 131104 | tf_op jit(solution)/shard_map/ppermute | solution.py:14
  72.6 10.0 %collective-permute-done.6 = bf16[3,1,128,512]{3,2,1,0:T(8,128)(2,1)S(1)} collective-permute-done((bf16[3,1,128,512]{3,2,1,0:T(8,128)(2,1)S(1)}, bf16[3,1,128,512]{3,2,1,0:T(8,128)(2,1)S(1)}, u32[]{:S(2)}, u32[]{:S(2)}) %collective-permute-start.6) | collective-permute-done | bytes 393248 | tf_op jit(solution)/shard_map/ppermute | solution.py:14
  82.7 6.9 %collective-permute-done.7 = bf16[3,1,128,512]{3,2,1,0:T(8,128)(2,1)S(1)} collective-permute-done((bf16[3,1,128,512]{3,2,1,0:T(8,128)(2,1)S(1)}, bf16[3,1,128,512]{3,2,1,0:T(8,128)(2,1)S(1)}, u32[]{:S(2)}, u32[]{:S(2)}) %collective-permute-start.7) | collective-permute-done | bytes 393248 | tf_op jit(solution)/shard_map/ppermute | solution.py:17
  93.6 3.5 %copy.20 = f32[12,512,128]{1,0,2:T(8,128)} copy(f32[12,512,128]{2,1,0:T(8,128)S(1)} %fusion.6) | data formatting | bytes 6291456 | tf_op jit(solution)/shard_map/tij,tjd->tid/dot_general | solution.py:70
  97.1 3.8 %fusion.19 = bf16[4,128,512]{2,0,1:T(4,128)(2,1)S(1)} fusion(f32[12,512,128]{1,0,2:T(8,128)} %copy.20, s32[12]{0:T(128)S(1)} %bitcast.123), kind=kOutput, calls=%fused_computation.23 | convolution fusion | flops 38010928 | bytes 3670064 | tf_op jit(solution)/shard_map/bt,tid->bid/dot_general | solution.py:74
  105.3 4.0 %reduce-scatter.6.cloned.1.call-done = bf16[256,512]{1,0:T(8,128)(2,1)} async-done(((bf16[512,512]{1,0:T(8,128)(2,1)}), bf16[256,512]{1,0:T(8,128)(2,1)}) %reduce-scatter.6.cloned.1.call-update) | async-done | bytes 262160 | tf_op jit(solution)/shard_map/reduce_scatter | solution.py:78
  109.3 2.4 %fusion.42 = (bf16[256,512]{1,0:T(8,128)(2,1)S(1)}, bf16[1,1,256,512]{3,2,1,0:T(8,128)(2,1)}) fusion(bf16[1,1,256,512]{3,2,1,0:T(8,128)(2,1)S(1)} %copy-done.19, f32[256]{0:T(256)S(1)} %copy-done.17, bf16[256,512]{1,0:T(8,128)(2,1)S(1)} %copy-done.3, bf16[2,512,512]{2,1,0:T(8,128)(2,1)} %multiply_convert_fusion, ...), kind=kOutput, calls=%fused_computation.54 | convolution fusion | flops 136839168 | bytes 2098176 | tf_op jit(solution)/shard_map/dot_general | solution.py:83
  112.7 2.3 %all_gather.3 = bf16[512,512]{1,0:T(8,128)(2,1)S(1)} all-gather(bf16[256,512]{1,0:T(8,128)(2,1)S(1)} %convolution_convert_fusion), channel_id=1, replica_groups=mesh['group'=2,'phi'=4,'eta'=2,'half'=2] {'half'}, dimensions={0}, use_global_device_ids=true | all-gather | bytes 786432 | tf_op jit(solution)/shard_map/all_gather | solution.py:99
  116.9 2.1 %fusion.10 = f32[12,512,128]{2,1,0:T(8,128)S(1)} fusion(bf16[12,128,512]{2,1,0:T(8,128)(2,1)} %gather_fusion, pred[12]{0:T(512)(128)(4,1)S(1)} %get-tuple-element.18, bf16[12]{0:T(256)(128)(2,1)S(1)} %get-tuple-element.17, bf16[1,1,12,128,128]{4,3,2,1,0:T(8,128)(2,1)S(1)} %copy-done), kind=kOutput, calls=%fused_computation.14 | convolution fusion | flops 202899456 | bytes 5111844 | tf_op jit(solution)/shard_map/tji,tjd->tid/dot_general | solution.py:107
  119.1 3.5 %copy.21 = f32[12,512,128]{1,0,2:T(8,128)} copy(f32[12,512,128]{2,1,0:T(8,128)S(1)} %fusion.10) | data formatting | bytes 6291456 | tf_op jit(solution)/shard_map/tji,tjd->tid/dot_general | solution.py:107
  122.6 3.7 %fusion = f32[6,128,512]{2,0,1:T(8,128)S(1)} fusion(f32[12,512,128]{1,0,2:T(8,128)} %copy.21, s32[12]{0:T(128)S(1)} %bitcast.124), kind=kOutput, calls=%fused_computation.3 | convolution fusion | flops 56623176 | bytes 4718640 | tf_op jit(solution)/shard_map/st,tid->sid/dot_general | solution.py:109
  127.4 3.8 %collective-permute-start.10 = (bf16[1,128,512]{2,1,0:T(8,128)(2,1)S(1)}, bf16[1,128,512]{2,1,0:T(8,128)(2,1)S(1)}, u32[]{:S(2)}, u32[]{:S(2)}) collective-permute-start(bf16[1,128,512]{2,1,0:T(8,128)(2,1)S(1)} %get-tuple-element.9), channel_id=1, source_target_pairs={{0,2},{1,3},{4,6},{5,7},{8,10},{9,11},{12,14},{13,15},{16,18},{17,... | collective-permute-start | bytes 393224 | tf_op jit(solution)/shard_map/ppermute | solution.py:14
  134.0 2.3 %collective-permute-start.9 = (bf16[1,128,512]{2,1,0:T(8,128)(2,1)S(1)}, bf16[1,128,512]{2,1,0:T(8,128)(2,1)S(1)}, u32[]{:S(2)}, u32[]{:S(2)}) collective-permute-start(bf16[1,128,512]{2,1,0:T(8,128)(2,1)S(1)} %get-tuple-element.10), channel_id=1, source_target_pairs={{4,0},{8,4},{12,8},{0,12},{5,1},{9,5},{13,9},{1,13},{6,2},{10,6},{... | collective-permute-start | bytes 393224 | tf_op jit(solution)/shard_map/ppermute | solution.py:17
  138.5 2.2 %collective-permute-done.8 = bf16[1,128,512]{2,1,0:T(8,128)(2,1)S(1)} collective-permute-done((bf16[1,128,512]{2,1,0:T(8,128)(2,1)S(1)}, bf16[1,128,512]{2,1,0:T(8,128)(2,1)S(1)}, u32[]{:S(2)}, u32[]{:S(2)}) %collective-permute-start.8) | collective-permute-done | bytes 131104 | tf_op jit(solution)/shard_map/ppermute | solution.py:14
  143.9 27.9 %reduce-scatter.8.cloned.1.call-done = bf16[2,128,512]{2,1,0:T(8,128)(2,1)} async-done(((bf16[2,512,512]{2,1,0:T(8,128)(2,1)}), bf16[2,128,512]{2,1,0:T(8,128)(2,1)}) %reduce-scatter.8.cloned.1.call-update) | async-done | bytes 262160 | tf_op jit(solution)/shard_map/reduce_scatter | solution.py:121
  171.8 32.9 %all-reduce.2.cloned.1.call-done = bf16[2,128,512]{2,1,0:T(8,128)(2,1)} async-done(((bf16[2,128,512]{2,1,0:T(8,128)(2,1)}), bf16[2,128,512]{2,1,0:T(8,128)(2,1)}) %all-reduce.2.cloned.1.call-update) | async-done | bytes 262160 | tf_op jit(solution)/shard_map/psum | solution.py:122
  (114 shorter events, 47.2 us)
Async XLA Ops:
  7.2 32.7 %copy-start = (bf16[1,1,12,128,128]{4,3,2,1,0:T(8,128)(2,1)S(1)}, bf16[1,1,12,128,128]{4,3,2,1,0:T(8,128)(2,1)}, u32[]{:S(2)}) copy-start(bf16[1,1,12,128,128]{4,3,2,1,0:T(8,128)(2,1)} %param.12) | copy-start | bytes 1179652
  7.2 51.5 %reduce-scatter.4.cloned.1.call-start = ((), (), s32[]{:S(2)}) async-start(), calls=%async_computation.3 | async-start | bytes 786432 | tf_op jit(solution)/shard_map/reduce_scatter | solution.py:78
  8.2 9.4 %collective-permute-start = (bf16[1,1,128,512]{3,2,1,0:T(8,128)(2,1)S(1)}, bf16[1,1,128,512]{3,2,1,0:T(8,128)(2,1)S(1)}, u32[]{:S(2)}, u32[]{:S(2)}) collective-permute-start(bf16[1,1,128,512]{3,2,1,0:T(8,128)(2,1)S(1)} %slice.89), channel_id=1, source_target_pairs={{0,4},{4,8},{8,12},{12,0},{1,5},{5,9},{9,13},{13,1},{2,6},{6,10},{... | collective-permute-start | bytes 393224 | tf_op jit(solution)/shard_map/ppermute | solution.py:14
  11.3 7.8 %collective-permute-start.1 = (bf16[1,1,128,512]{3,2,1,0:T(8,128)(2,1)S(1)}, bf16[1,1,128,512]{3,2,1,0:T(8,128)(2,1)S(1)}, u32[]{:S(2)}, u32[]{:S(2)}) collective-permute-start(bf16[1,1,128,512]{3,2,1,0:T(8,128)(2,1)S(1)} %slice.89), channel_id=1, source_target_pairs={{4,0},{8,4},{12,8},{0,12},{5,1},{9,5},{13,9},{1,13},{6,2},{10,6},{... | collective-permute-start | bytes 393224 | tf_op jit(solution)/shard_map/ppermute | solution.py:17
  14.7 25.2 %copy-start.16 = (pred[12]{0:T(512)(128)(4,1)}, pred[12]{0:T(512)(128)(4,1)S(1)}, u32[]{:S(2)}) copy-start(pred[12]{0:T(512)(128)(4,1)S(1)} %compare_and_fusion) | copy-start | bytes 40
  19.1 12.1 %collective-permute-start.2 = (bf16[3,1,128,512]{3,2,1,0:T(8,128)(2,1)S(1)}, bf16[3,1,128,512]{3,2,1,0:T(8,128)(2,1)S(1)}, u32[]{:S(2)}, u32[]{:S(2)}) collective-permute-start(bf16[3,1,128,512]{3,2,1,0:T(8,128)(2,1)S(1)} %pad_maximum_fusion.1), channel_id=1, source_target_pairs={{0,2},{2,0},{1,3},{3,1},{4,6},{6,4},{5,7},{7,5},{8,10},{10,8},{9,1... | collective-permute-start | bytes 1179656 | tf_op jit(solution)/shard_map/ppermute | solution.py:14
  20.6 17.4 %collective-permute-start.3 = (bf16[3,1,128,512]{3,2,1,0:T(8,128)(2,1)S(1)}, bf16[3,1,128,512]{3,2,1,0:T(8,128)(2,1)S(1)}, u32[]{:S(2)}, u32[]{:S(2)}) collective-permute-start(bf16[3,1,128,512]{3,2,1,0:T(8,128)(2,1)S(1)} %pad_maximum_fusion.1), channel_id=1, source_target_pairs={{2,0},{0,2},{3,1},{1,3},{6,4},{4,6},{7,5},{5,7},{10,8},{8,10},{11,... | collective-permute-start | bytes 1179656 | tf_op jit(solution)/shard_map/ppermute | solution.py:17
  50.2 59.1 %reduce-scatter.6.cloned.1.call-start = ((), (), s32[]{:S(2)}) async-start(), calls=%async_computation.4 | async-start | bytes 786432 | tf_op jit(solution)/shard_map/reduce_scatter | solution.py:78
  61.1 21.6 %copy-start.2 = (bf16[256,512]{1,0:T(8,128)(2,1)}, bf16[256,512]{1,0:T(8,128)(2,1)S(1)}, u32[]{:S(2)}) copy-start(bf16[256,512]{1,0:T(8,128)(2,1)S(1)} %get-tuple-element.19) | copy-start | bytes 786436
  61.1 8.3 %collective-permute-start.4 = (bf16[1,1,128,512]{3,2,1,0:T(8,128)(2,1)S(1)}, bf16[1,1,128,512]{3,2,1,0:T(8,128)(2,1)S(1)}, u32[]{:S(2)}, u32[]{:S(2)}) collective-permute-start(bf16[1,1,128,512]{3,2,1,0:T(8,128)(2,1)S(1)} %slice_bitcast_fusion.6), channel_id=1, source_target_pairs={{0,4},{4,8},{8,12},{12,0},{1,5},{5,9},{9,13},{13,1},{2,6},{6,10},{... | collective-permute-start | bytes 393224 | tf_op jit(solution)/shard_map/ppermute | solution.py:14
  62.9 7.6 %collective-permute-start.5 = (bf16[1,1,128,512]{3,2,1,0:T(8,128)(2,1)S(1)}, bf16[1,1,128,512]{3,2,1,0:T(8,128)(2,1)S(1)}, u32[]{:S(2)}, u32[]{:S(2)}) collective-permute-start(bf16[1,1,128,512]{3,2,1,0:T(8,128)(2,1)S(1)} %slice_bitcast_fusion.6), channel_id=1, source_target_pairs={{4,0},{8,4},{12,8},{0,12},{5,1},{9,5},{13,9},{1,13},{6,2},{10,6},{... | collective-permute-start | bytes 393224 | tf_op jit(solution)/shard_map/ppermute | solution.py:17
  70.5 12.1 %collective-permute-start.6 = (bf16[3,1,128,512]{3,2,1,0:T(8,128)(2,1)S(1)}, bf16[3,1,128,512]{3,2,1,0:T(8,128)(2,1)S(1)}, u32[]{:S(2)}, u32[]{:S(2)}) collective-permute-start(bf16[3,1,128,512]{3,2,1,0:T(8,128)(2,1)S(1)} %pad_maximum_fusion.2), channel_id=1, source_target_pairs={{0,2},{2,0},{1,3},{3,1},{4,6},{6,4},{5,7},{7,5},{8,10},{10,8},{9,1... | collective-permute-start | bytes 1179656 | tf_op jit(solution)/shard_map/ppermute | solution.py:14
  72.0 17.5 %collective-permute-start.7 = (bf16[3,1,128,512]{3,2,1,0:T(8,128)(2,1)S(1)}, bf16[3,1,128,512]{3,2,1,0:T(8,128)(2,1)S(1)}, u32[]{:S(2)}, u32[]{:S(2)}) collective-permute-start(bf16[3,1,128,512]{3,2,1,0:T(8,128)(2,1)S(1)} %pad_maximum_fusion.2), channel_id=1, source_target_pairs={{2,0},{0,2},{3,1},{1,3},{6,4},{4,6},{7,5},{5,7},{10,8},{8,10},{11,... | collective-permute-start | bytes 1179656 | tf_op jit(solution)/shard_map/ppermute | solution.py:17
  101.8 70.0 %reduce-scatter.8.cloned.1.call-start = ((), (), s32[]{:S(2)}) async-start(), calls=%async_computation.5 | async-start | bytes 1310720 | tf_op jit(solution)/shard_map/reduce_scatter | solution.py:121
  105.2 6.4 %copy-start.7 = (bf16[2,512,512]{2,1,0:T(8,128)(2,1)S(1)}, bf16[2,512,512]{2,1,0:T(8,128)(2,1)}, u32[]{:S(2)}) copy-start(bf16[2,512,512]{2,1,0:T(8,128)(2,1)} %multiply_convert_fusion) | copy-start | bytes 3145732
  127.3 9.1 %copy-start.1 = (f32[512,512]{1,0:T(8,128)S(1)}, f32[512,512]{1,0:T(8,128)}, u32[]{:S(2)}) copy-start(f32[512,512]{1,0:T(8,128)} %squeeze.39) | copy-start | bytes 3145732
  127.3 9.1 %copy-start.4 = (bf16[256,512]{1,0:T(8,128)(2,1)S(1)}, bf16[256,512]{1,0:T(8,128)(2,1)}, u32[]{:S(2)}) copy-start(bf16[256,512]{1,0:T(8,128)(2,1)} %copy-done.2) | copy-start | bytes 786436
  127.3 9.1 %copy-start.11 = (bf16[256,512]{1,0:T(8,128)(2,1)S(1)}, bf16[256,512]{1,0:T(8,128)(2,1)}, u32[]{:S(2)}) copy-start(bf16[256,512]{1,0:T(8,128)(2,1)} %reduce-scatter.6.cloned.1.call-done) | copy-start | bytes 786436
  127.3 9.0 %copy-start.13 = (bf16[256,512]{1,0:T(8,128)(2,1)S(1)}, bf16[256,512]{1,0:T(8,128)(2,1)}, u32[]{:S(2)}) copy-start(bf16[256,512]{1,0:T(8,128)(2,1)} %copy-done.12) | copy-start | bytes 786436
  127.4 9.4 %collective-permute-start.10 = (bf16[1,128,512]{2,1,0:T(8,128)(2,1)S(1)}, bf16[1,128,512]{2,1,0:T(8,128)(2,1)S(1)}, u32[]{:S(2)}, u32[]{:S(2)}) collective-permute-start(bf16[1,128,512]{2,1,0:T(8,128)(2,1)S(1)} %get-tuple-element.9), channel_id=1, source_target_pairs={{0,2},{1,3},{4,6},{5,7},{8,10},{9,11},{12,14},{13,15},{16,18},{17,... | collective-permute-start | bytes 393224 | tf_op jit(solution)/shard_map/ppermute | solution.py:14
  131.1 7.3 %collective-permute-start.11 = (bf16[1,128,512]{2,1,0:T(8,128)(2,1)S(1)}, bf16[1,128,512]{2,1,0:T(8,128)(2,1)S(1)}, u32[]{:S(2)}, u32[]{:S(2)}) collective-permute-start(bf16[1,128,512]{2,1,0:T(8,128)(2,1)S(1)} %get-tuple-element.8), channel_id=1, source_target_pairs={{2,0},{3,1},{6,4},{7,5},{10,8},{11,9},{14,12},{15,13},{18,16},{19,... | collective-permute-start | bytes 393224 | tf_op jit(solution)/shard_map/ppermute | solution.py:17
  132.4 8.2 %collective-permute-start.8 = (bf16[1,128,512]{2,1,0:T(8,128)(2,1)S(1)}, bf16[1,128,512]{2,1,0:T(8,128)(2,1)S(1)}, u32[]{:S(2)}, u32[]{:S(2)}) collective-permute-start(bf16[1,128,512]{2,1,0:T(8,128)(2,1)S(1)} %get-tuple-element.7), channel_id=1, source_target_pairs={{0,4},{4,8},{8,12},{12,0},{1,5},{5,9},{9,13},{13,1},{2,6},{6,10},{... | collective-permute-start | bytes 393224 | tf_op jit(solution)/shard_map/ppermute | solution.py:14
  134.0 8.0 %collective-permute-start.9 = (bf16[1,128,512]{2,1,0:T(8,128)(2,1)S(1)}, bf16[1,128,512]{2,1,0:T(8,128)(2,1)S(1)}, u32[]{:S(2)}, u32[]{:S(2)}) collective-permute-start(bf16[1,128,512]{2,1,0:T(8,128)(2,1)S(1)} %get-tuple-element.10), channel_id=1, source_target_pairs={{4,0},{8,4},{12,8},{0,12},{5,1},{9,5},{13,9},{1,13},{6,2},{10,6},{... | collective-permute-start | bytes 393224 | tf_op jit(solution)/shard_map/ppermute | solution.py:17
  143.8 60.8 %all-reduce.2.cloned.1.call-start = ((), (), s32[]{:S(2)}) async-start(), calls=%async_computation.6 | async-start | bytes 524288 | tf_op jit(solution)/shard_map/psum | solution.py:122
  (15 other events, 68.0 us)
Sparse Core Ops, SparseCore 0:
  50.3 7.6 reduce-scatter.3
  101.9 7.3 reduce-scatter.5
  143.9 27.7 reduce-scatter.7
  174.0 30.5 all-reduce.1
where the time goes:
time: 214 us; the launch traced here: 213 us
  waiting for transfers between devices  113 us (53%)
  local copies, waits for them, and re-layouts  29.8 us (14%)
  matrix products  23.7 us (11%)
  starting transfers between devices  22.3 us (10%)
  between operations  14.9 us (7%)
  other arithmetic  7.39 us (3%)
  blocking collectives  2.35 us (1%)
    psum x1, waiting for transfers between devices, body(): result = lax.psum(shares, ('eta', 'half')).astype(jnp.float32)  32.9 us
    ppermute x6, waiting for transfers between devices, with_halo(): lax.ppermute(lax.slice_in_dim(block, block.shape[dim] - width, None, axis...  28.5 us
    reduce_scatter x1, waiting for transfers between devices, body(): lax.psum_scatter(stacked.astype(jnp.bfloat16), 'phi', scatter_dimension=1...  27.9 us
    ppermute x6, waiting for transfers between devices, with_halo(): lax.ppermute(lax.slice_in_dim(block, 0, width, axis=dim), axis, backward)  19.2 us
    ppermute x6, starting transfers between devices, with_halo(): lax.ppermute(lax.slice_in_dim(block, block.shape[dim] - width, None, axis...  13.3 us
    ppermute x6, starting transfers between devices, with_halo(): lax.ppermute(lax.slice_in_dim(block, 0, width, axis=dim), axis, backward)  8.89 us
    dot_general x2, matrix products, body(): jnp.einsum('bt,tid->bid', messages_onehot, messages_parts, precision=lax....  7.58 us
    dot_general x2, local copies, waits for them, and re-layouts, body(): jnp.einsum('tij,tjd->tid', tile_set, messages_picked, preferred_element_t...  6.92 us
  transfers between devices with their start and end apart: 16, of which 14 were waited for; matrix products, arithmetic and copies ran while one was open for 7% of the time, Pallas kernels for 0%

commit v1 on v0

--- a/solution.py
+++ b/solution.py
@@ -2,6 +2,11 @@
 import jax.numpy as jnp
 from jax import lax
 from jax.sharding import PartitionSpec as P
+
+
+def matrix_test(local_values, mesh_dim, bus_axis):
+    res = lax.psum(lax.psum(local_values, mesh_dim), bus_axis)
+    return res
 
 
 def with_halo(block, sides, width, periodic):
@@ -119,7 +124,7 @@
             upstream = live * upstream + back.astype(jnp.float32) + own
     stacked = jnp.stack(partials)
     shares = lax.psum_scatter(stacked.astype(jnp.bfloat16), "phi", scatter_dimension=1, tiled=True)
-    result = lax.psum(shares, ("eta", "half")).astype(jnp.float32)
+    result = matrix_test(shares, "half", "eta").astype(jnp.float32)
     return (state[None, None], result)
 
 

time: 214 us -> 226 us (1.056)
  waiting for transfers between devices: 113 us -> 125 us
    psum x1 -> x2, waiting for transfers between devices: 32.9 us -> 45.7 us  [matrix_test(): res = lax.psum(lax.psum(local_values, mesh_dim), bus_axis)]
  transfers between devices with their start and end apart: 16 -> 17, of which waited for: 14 -> 15; matrix products, arithmetic and copies ran while one was open for 7% -> 6% of each run, Pallas kernels for 0% -> 0%
where the time goes in v1:
time: 226 us
  waiting for transfers between devices  125 us (55%)
  local copies, waits for them, and re-layouts  29.8 us (13%)
  matrix products  23.7 us (10%)
  starting transfers between devices  22.4 us (10%)
  between operations  14.9 us (7%)
  other arithmetic  7.39 us (3%)
  blocking collectives  2.35 us (1%)
    psum x2, waiting for transfers between devices, matrix_test(): res = lax.psum(lax.psum(local_values, mesh_dim), bus_axis)  45.7 us
    ppermute x6, waiting for transfers between devices, with_halo(): lax.ppermute(lax.slice_in_dim(block, block.shape[dim] - width, None, axis...  28.5 us
    reduce_scatter x1, waiting for transfers between devices, body(): lax.psum_scatter(stacked.astype(jnp.bfloat16), 'phi', scatter_dimension=1...  27.9 us
    ppermute x6, waiting for transfers between devices, with_halo(): lax.ppermute(lax.slice_in_dim(block, 0, width, axis=dim), axis, backward)  19.2 us
    ppermute x6, starting transfers between devices, with_halo(): lax.ppermute(lax.slice_in_dim(block, block.shape[dim] - width, None, axis...  13.3 us
    ppermute x6, starting transfers between devices, with_halo(): lax.ppermute(lax.slice_in_dim(block, 0, width, axis=dim), axis, backward)  8.89 us
    dot_general x2, matrix products, body(): jnp.einsum('bt,tid->bid', messages_onehot, messages_parts, precision=lax....  7.58 us
    dot_general x2, local copies, waits for them, and re-layouts, body(): jnp.einsum('tij,tjd->tid', tile_set, messages_picked, preferred_element_t...  6.92 us
  transfers between devices with their start and end apart: 17, of which 15 were waited for; matrix products, arithmetic and copies ran while one was open for 6% of the time, Pallas kernels for 0%

profile of v1, /device:TPU:0, one launch (start us, length us, event | category | flops | bytes accessed | tf_op | source)
XLA Modules:
  0.0 225.8 jit_solution(17761203293222671230)
XLA Ops:
  8.2 3.1 %collective-permute-start = (bf16[1,1,128,512]{3,2,1,0:T(8,128)(2,1)S(1)}, bf16[1,1,128,512]{3,2,1,0:T(8,128)(2,1)S(1)}, u32[]{:S(2)}, u32[]{:S(2)}) collective-permute-start(bf16[1,1,128,512]{3,2,1,0:T(8,128)(2,1)S(1)} %slice.89), channel_id=1, source_target_pairs={{0,4},{4,8},{8,12},{12,0},{1,5},{5,9},{9,13},{13,1},{2,6},{6,10},{... | collective-permute-start | bytes 393224 | tf_op jit(solution)/shard_map/ppermute | solution.py:19
  21.2 10.0 %collective-permute-done.2 = bf16[3,1,128,512]{3,2,1,0:T(8,128)(2,1)S(1)} collective-permute-done((bf16[3,1,128,512]{3,2,1,0:T(8,128)(2,1)S(1)}, bf16[3,1,128,512]{3,2,1,0:T(8,128)(2,1)S(1)}, u32[]{:S(2)}, u32[]{:S(2)}) %collective-permute-start.2) | collective-permute-done | bytes 393248 | tf_op jit(solution)/shard_map/ppermute | solution.py:19
  31.2 6.8 %collective-permute-done.3 = bf16[3,1,128,512]{3,2,1,0:T(8,128)(2,1)S(1)} collective-permute-done((bf16[3,1,128,512]{3,2,1,0:T(8,128)(2,1)S(1)}, bf16[3,1,128,512]{3,2,1,0:T(8,128)(2,1)S(1)}, u32[]{:S(2)}, u32[]{:S(2)}) %collective-permute-start.3) | collective-permute-done | bytes 393248 | tf_op jit(solution)/shard_map/ppermute | solution.py:22
  42.0 3.5 %copy.19 = f32[12,512,128]{1,0,2:T(8,128)} copy(f32[12,512,128]{2,1,0:T(8,128)S(1)} %fusion.8) | data formatting | bytes 6291456 | tf_op jit(solution)/shard_map/tij,tjd->tid/dot_general | solution.py:75
  45.5 3.8 %fusion.16 = bf16[4,128,512]{2,0,1:T(4,128)(2,1)S(1)} fusion(f32[12,512,128]{1,0,2:T(8,128)} %copy.19, s32[12]{0:T(128)S(1)} %bitcast.122), kind=kOutput, calls=%fused_computation.22 | convolution fusion | flops 38010928 | bytes 3670064 | tf_op jit(solution)/shard_map/bt,tid->bid/dot_general | solution.py:79
  50.3 2.3 %broadcast_in_dim.41 = f32[2,8,64,8,64]{4,3,2,1,0:T(8,128)} broadcast(f32[2,8,8]{2,1,0:T(8,128)S(1)} %convert_element_type.115), dimensions={0,1,3} | broadcast | bytes 2097664 | tf_op jit(solution)/shard_map/broadcast_in_dim | solution.py:54
  52.6 3.5 %convert_element_type.116 = f32[2,512,512]{2,1,0:T(8,128)S(1)} reshape(f32[2,8,64,8,64]{4,3,2,1,0:T(8,128)} %broadcast_in_dim.41) | data formatting | bytes 4194304 | tf_op jit(solution)/shard_map/convert_element_type | solution.py:56
  58.7 2.4 %fusion.35 = (bf16[256,512]{1,0:T(8,128)(2,1)S(1)}, f32[256,512]{1,0:T(8,128)}) fusion(bf16[1,1,256,512]{3,2,1,0:T(8,128)(2,1)} %param.10, f32[256]{0:T(256)} %compare_convert_fusion.1, bf16[2,512,512]{2,1,0:T(8,128)(2,1)} %multiply_convert_fusion, bf16[256,512]{1,0:T(8,128)(2,1)} %reduce-scatter.4.cloned.1.call-done), kind=kOutput, calls=%fused_computation.43 | convolution fusion | flops 135790592 | bytes 2098176 | tf_op jit(solution)/shard_map/dot_general | solution.py:88
  65.0 4.4 %collective-permute-done.4 = bf16[1,1,128,512]{3,2,1,0:T(8,128)(2,1)S(1)} collective-permute-done((bf16[1,1,128,512]{3,2,1,0:T(8,128)(2,1)S(1)}, bf16[1,1,128,512]{3,2,1,0:T(8,128)(2,1)S(1)}, u32[]{:S(2)}, u32[]{:S(2)}) %collective-permute-start.4) | collective-permute-done | bytes 131104 | tf_op jit(solution)/shard_map/ppermute | solution.py:19
  72.6 10.0 %collective-permute-done.6 = bf16[3,1,128,512]{3,2,1,0:T(8,128)(2,1)S(1)} collective-permute-done((bf16[3,1,128,512]{3,2,1,0:T(8,128)(2,1)S(1)}, bf16[3,1,128,512]{3,2,1,0:T(8,128)(2,1)S(1)}, u32[]{:S(2)}, u32[]{:S(2)}) %collective-permute-start.6) | collective-permute-done | bytes 393248 | tf_op jit(solution)/shard_map/ppermute | solution.py:19
  82.7 6.9 %collective-permute-done.7 = bf16[3,1,128,512]{3,2,1,0:T(8,128)(2,1)S(1)} collective-permute-done((bf16[3,1,128,512]{3,2,1,0:T(8,128)(2,1)S(1)}, bf16[3,1,128,512]{3,2,1,0:T(8,128)(2,1)S(1)}, u32[]{:S(2)}, u32[]{:S(2)}) %collective-permute-start.7) | collective-permute-done | bytes 393248 | tf_op jit(solution)/shard_map/ppermute | solution.py:22
  93.6 3.5 %copy.20 = f32[12,512,128]{1,0,2:T(8,128)} copy(f32[12,512,128]{2,1,0:T(8,128)S(1)} %fusion.6) | data formatting | bytes 6291456 | tf_op jit(solution)/shard_map/tij,tjd->tid/dot_general | solution.py:75
  97.1 3.8 %fusion.19 = bf16[4,128,512]{2,0,1:T(4,128)(2,1)S(1)} fusion(f32[12,512,128]{1,0,2:T(8,128)} %copy.20, s32[12]{0:T(128)S(1)} %bitcast.123), kind=kOutput, calls=%fused_computation.23 | convolution fusion | flops 38010928 | bytes 3670064 | tf_op jit(solution)/shard_map/bt,tid->bid/dot_general | solution.py:79
  105.3 4.0 %reduce-scatter.6.cloned.1.call-done = bf16[256,512]{1,0:T(8,128)(2,1)} async-done(((bf16[512,512]{1,0:T(8,128)(2,1)}), bf16[256,512]{1,0:T(8,128)(2,1)}) %reduce-scatter.6.cloned.1.call-update) | async-done | bytes 262160 | tf_op jit(solution)/shard_map/reduce_scatter | solution.py:83
  109.3 2.4 %fusion.42 = (bf16[256,512]{1,0:T(8,128)(2,1)S(1)}, bf16[1,1,256,512]{3,2,1,0:T(8,128)(2,1)}) fusion(bf16[1,1,256,512]{3,2,1,0:T(8,128)(2,1)S(1)} %copy-done.19, f32[256]{0:T(256)S(1)} %copy-done.17, bf16[256,512]{1,0:T(8,128)(2,1)S(1)} %copy-done.3, bf16[2,512,512]{2,1,0:T(8,128)(2,1)} %multiply_convert_fusion, ...), kind=kOutput, calls=%fused_computation.54 | convolution fusion | flops 136839168 | bytes 2098176 | tf_op jit(solution)/shard_map/dot_general | solution.py:88
  112.7 2.3 %all_gather.3 = bf16[512,512]{1,0:T(8,128)(2,1)S(1)} all-gather(bf16[256,512]{1,0:T(8,128)(2,1)S(1)} %convolution_convert_fusion), channel_id=1, replica_groups=mesh['group'=2,'phi'=4,'eta'=2,'half'=2] {'half'}, dimensions={0}, use_global_device_ids=true | all-gather | bytes 786432 | tf_op jit(solution)/shard_map/all_gather | solution.py:104
  119.1 3.5 %copy.21 = f32[12,512,128]{1,0,2:T(8,128)} copy(f32[12,512,128]{2,1,0:T(8,128)S(1)} %fusion.10) | data formatting | bytes 6291456 | tf_op jit(solution)/shard_map/tji,tjd->tid/dot_general | solution.py:112
  122.6 3.7 %fusion = f32[6,128,512]{2,0,1:T(8,128)S(1)} fusion(f32[12,512,128]{1,0,2:T(8,128)} %copy.21, s32[12]{0:T(128)S(1)} %bitcast.124), kind=kOutput, calls=%fused_computation.3 | convolution fusion | flops 56623176 | bytes 4718640 | tf_op jit(solution)/shard_map/st,tid->sid/dot_general | solution.py:114
  127.4 3.8 %collective-permute-start.10 = (bf16[1,128,512]{2,1,0:T(8,128)(2,1)S(1)}, bf16[1,128,512]{2,1,0:T(8,128)(2,1)S(1)}, u32[]{:S(2)}, u32[]{:S(2)}) collective-permute-start(bf16[1,128,512]{2,1,0:T(8,128)(2,1)S(1)} %get-tuple-element.9), channel_id=1, source_target_pairs={{0,2},{1,3},{4,6},{5,7},{8,10},{9,11},{12,14},{13,15},{16,18},{17,... | collective-permute-start | bytes 393224 | tf_op jit(solution)/shard_map/ppermute | solution.py:19
  134.0 2.3 %collective-permute-start.9 = (bf16[1,128,512]{2,1,0:T(8,128)(2,1)S(1)}, bf16[1,128,512]{2,1,0:T(8,128)(2,1)S(1)}, u32[]{:S(2)}, u32[]{:S(2)}) collective-permute-start(bf16[1,128,512]{2,1,0:T(8,128)(2,1)S(1)} %get-tuple-element.10), channel_id=1, source_target_pairs={{4,0},{8,4},{12,8},{0,12},{5,1},{9,5},{13,9},{1,13},{6,2},{10,6},{... | collective-permute-start | bytes 393224 | tf_op jit(solution)/shard_map/ppermute | solution.py:22
  138.5 2.2 collective-permute-done.8
  143.9 27.9 %reduce-scatter.8.cloned.1.call-done = bf16[2,128,512]{2,1,0:T(8,128)(2,1)} async-done(((bf16[2,512,512]{2,1,0:T(8,128)(2,1)}), bf16[2,128,512]{2,1,0:T(8,128)(2,1)}) %reduce-scatter.8.cloned.1.call-update) | async-done | bytes 262160 | tf_op jit(solution)/shard_map/reduce_scatter | solution.py:126
  171.8 19.2 %all-reduce.3.cloned.1.call-done = bf16[2,128,512]{2,1,0:T(8,128)(2,1)} async-done(((bf16[2,128,512]{2,1,0:T(8,128)(2,1)}), bf16[2,128,512]{2,1,0:T(8,128)(2,1)}) %all-reduce.3.cloned.1.call-update) | async-done | bytes 262160 | tf_op jit(solution)/shard_map/psum | solution.py:8
  191.0 26.5 %all-reduce.5.cloned.1.call-done = bf16[2,128,512]{2,1,0:T(8,128)(2,1)} async-done(((bf16[2,128,512]{2,1,0:T(8,128)(2,1)}), bf16[2,128,512]{2,1,0:T(8,128)(2,1)}) %all-reduce.5.cloned.1.call-update) | async-done | bytes 262160 | tf_op jit(solution)/shard_map/psum | solution.py:8
  (117 shorter events, 49.4 us)
Async XLA Ops:
  7.2 32.7 %copy-start = (bf16[1,1,12,128,128]{4,3,2,1,0:T(8,128)(2,1)S(1)}, bf16[1,1,12,128,128]{4,3,2,1,0:T(8,128)(2,1)}, u32[]{:S(2)}) copy-start(bf16[1,1,12,128,128]{4,3,2,1,0:T(8,128)(2,1)} %param.12) | copy-start | bytes 1179652
  7.2 51.5 %reduce-scatter.4.cloned.1.call-start = ((), (), s32[]{:S(2)}) async-start(), calls=%async_computation.3 | async-start | bytes 786432 | tf_op jit(solution)/shard_map/reduce_scatter | solution.py:83
  8.2 9.4 %collective-permute-start = (bf16[1,1,128,512]{3,2,1,0:T(8,128)(2,1)S(1)}, bf16[1,1,128,512]{3,2,1,0:T(8,128)(2,1)S(1)}, u32[]{:S(2)}, u32[]{:S(2)}) collective-permute-start(bf16[1,1,128,512]{3,2,1,0:T(8,128)(2,1)S(1)} %slice.89), channel_id=1, source_target_pairs={{0,4},{4,8},{8,12},{12,0},{1,5},{5,9},{9,13},{13,1},{2,6},{6,10},{... | collective-permute-start | bytes 393224 | tf_op jit(solution)/shard_map/ppermute | solution.py:19
  11.3 7.8 %collective-permute-start.1 = (bf16[1,1,128,512]{3,2,1,0:T(8,128)(2,1)S(1)}, bf16[1,1,128,512]{3,2,1,0:T(8,128)(2,1)S(1)}, u32[]{:S(2)}, u32[]{:S(2)}) collective-permute-start(bf16[1,1,128,512]{3,2,1,0:T(8,128)(2,1)S(1)} %slice.89), channel_id=1, source_target_pairs={{4,0},{8,4},{12,8},{0,12},{5,1},{9,5},{13,9},{1,13},{6,2},{10,6},{... | collective-permute-start | bytes 393224 | tf_op jit(solution)/shard_map/ppermute | solution.py:22
  14.7 25.2 %copy-start.16 = (pred[12]{0:T(512)(128)(4,1)}, pred[12]{0:T(512)(128)(4,1)S(1)}, u32[]{:S(2)}) copy-start(pred[12]{0:T(512)(128)(4,1)S(1)} %compare_and_fusion) | copy-start | bytes 40
  19.1 12.1 %collective-permute-start.2 = (bf16[3,1,128,512]{3,2,1,0:T(8,128)(2,1)S(1)}, bf16[3,1,128,512]{3,2,1,0:T(8,128)(2,1)S(1)}, u32[]{:S(2)}, u32[]{:S(2)}) collective-permute-start(bf16[3,1,128,512]{3,2,1,0:T(8,128)(2,1)S(1)} %pad_maximum_fusion.1), channel_id=1, source_target_pairs={{0,2},{2,0},{1,3},{3,1},{4,6},{6,4},{5,7},{7,5},{8,10},{10,8},{9,1... | collective-permute-start | bytes 1179656 | tf_op jit(solution)/shard_map/ppermute | solution.py:19
  20.6 17.4 %collective-permute-start.3 = (bf16[3,1,128,512]{3,2,1,0:T(8,128)(2,1)S(1)}, bf16[3,1,128,512]{3,2,1,0:T(8,128)(2,1)S(1)}, u32[]{:S(2)}, u32[]{:S(2)}) collective-permute-start(bf16[3,1,128,512]{3,2,1,0:T(8,128)(2,1)S(1)} %pad_maximum_fusion.1), channel_id=1, source_target_pairs={{2,0},{0,2},{3,1},{1,3},{6,4},{4,6},{7,5},{5,7},{10,8},{8,10},{11,... | collective-permute-start | bytes 1179656 | tf_op jit(solution)/shard_map/ppermute | solution.py:22
  50.2 59.1 %reduce-scatter.6.cloned.1.call-start = ((), (), s32[]{:S(2)}) async-start(), calls=%async_computation.4 | async-start | bytes 786432 | tf_op jit(solution)/shard_map/reduce_scatter | solution.py:83
  61.1 21.6 %copy-start.2 = (bf16[256,512]{1,0:T(8,128)(2,1)}, bf16[256,512]{1,0:T(8,128)(2,1)S(1)}, u32[]{:S(2)}) copy-start(bf16[256,512]{1,0:T(8,128)(2,1)S(1)} %get-tuple-element.19) | copy-start | bytes 786436
  61.1 8.3 %collective-permute-start.4 = (bf16[1,1,128,512]{3,2,1,0:T(8,128)(2,1)S(1)}, bf16[1,1,128,512]{3,2,1,0:T(8,128)(2,1)S(1)}, u32[]{:S(2)}, u32[]{:S(2)}) collective-permute-start(bf16[1,1,128,512]{3,2,1,0:T(8,128)(2,1)S(1)} %slice_bitcast_fusion.6), channel_id=1, source_target_pairs={{0,4},{4,8},{8,12},{12,0},{1,5},{5,9},{9,13},{13,1},{2,6},{6,10},{... | collective-permute-start | bytes 393224 | tf_op jit(solution)/shard_map/ppermute | solution.py:19
  62.9 7.6 %collective-permute-start.5 = (bf16[1,1,128,512]{3,2,1,0:T(8,128)(2,1)S(1)}, bf16[1,1,128,512]{3,2,1,0:T(8,128)(2,1)S(1)}, u32[]{:S(2)}, u32[]{:S(2)}) collective-permute-start(bf16[1,1,128,512]{3,2,1,0:T(8,128)(2,1)S(1)} %slice_bitcast_fusion.6), channel_id=1, source_target_pairs={{4,0},{8,4},{12,8},{0,12},{5,1},{9,5},{13,9},{1,13},{6,2},{10,6},{... | collective-permute-start | bytes 393224 | tf_op jit(solution)/shard_map/ppermute | solution.py:22
  70.5 12.1 %collective-permute-start.6 = (bf16[3,1,128,512]{3,2,1,0:T(8,128)(2,1)S(1)}, bf16[3,1,128,512]{3,2,1,0:T(8,128)(2,1)S(1)}, u32[]{:S(2)}, u32[]{:S(2)}) collective-permute-start(bf16[3,1,128,512]{3,2,1,0:T(8,128)(2,1)S(1)} %pad_maximum_fusion.2), channel_id=1, source_target_pairs={{0,2},{2,0},{1,3},{3,1},{4,6},{6,4},{5,7},{7,5},{8,10},{10,8},{9,1... | collective-permute-start | bytes 1179656 | tf_op jit(solution)/shard_map/ppermute | solution.py:19
  72.0 17.5 %collective-permute-start.7 = (bf16[3,1,128,512]{3,2,1,0:T(8,128)(2,1)S(1)}, bf16[3,1,128,512]{3,2,1,0:T(8,128)(2,1)S(1)}, u32[]{:S(2)}, u32[]{:S(2)}) collective-permute-start(bf16[3,1,128,512]{3,2,1,0:T(8,128)(2,1)S(1)} %pad_maximum_fusion.2), channel_id=1, source_target_pairs={{2,0},{0,2},{3,1},{1,3},{6,4},{4,6},{7,5},{5,7},{10,8},{8,10},{11,... | collective-permute-start | bytes 1179656 | tf_op jit(solution)/shard_map/ppermute | solution.py:22
  101.8 70.0 %reduce-scatter.8.cloned.1.call-start = ((), (), s32[]{:S(2)}) async-start(), calls=%async_computation.5 | async-start | bytes 1310720 | tf_op jit(solution)/shard_map/reduce_scatter | solution.py:126
  127.3 9.1 %copy-start.1 = (f32[512,512]{1,0:T(8,128)S(1)}, f32[512,512]{1,0:T(8,128)}, u32[]{:S(2)}) copy-start(f32[512,512]{1,0:T(8,128)} %squeeze.39) | copy-start | bytes 3145732
  127.3 9.1 %copy-start.4 = (bf16[256,512]{1,0:T(8,128)(2,1)S(1)}, bf16[256,512]{1,0:T(8,128)(2,1)}, u32[]{:S(2)}) copy-start(bf16[256,512]{1,0:T(8,128)(2,1)} %copy-done.2) | copy-start | bytes 786436
  127.3 9.1 %copy-start.11 = (bf16[256,512]{1,0:T(8,128)(2,1)S(1)}, bf16[256,512]{1,0:T(8,128)(2,1)}, u32[]{:S(2)}) copy-start(bf16[256,512]{1,0:T(8,128)(2,1)} %reduce-scatter.6.cloned.1.call-done) | copy-start | bytes 786436
  127.3 9.0 %copy-start.13 = (bf16[256,512]{1,0:T(8,128)(2,1)S(1)}, bf16[256,512]{1,0:T(8,128)(2,1)}, u32[]{:S(2)}) copy-start(bf16[256,512]{1,0:T(8,128)(2,1)} %copy-done.12) | copy-start | bytes 786436
  127.4 9.4 %collective-permute-start.10 = (bf16[1,128,512]{2,1,0:T(8,128)(2,1)S(1)}, bf16[1,128,512]{2,1,0:T(8,128)(2,1)S(1)}, u32[]{:S(2)}, u32[]{:S(2)}) collective-permute-start(bf16[1,128,512]{2,1,0:T(8,128)(2,1)S(1)} %get-tuple-element.9), channel_id=1, source_target_pairs={{0,2},{1,3},{4,6},{5,7},{8,10},{9,11},{12,14},{13,15},{16,18},{17,... | collective-permute-start | bytes 393224 | tf_op jit(solution)/shard_map/ppermute | solution.py:19
  131.1 7.3 %collective-permute-start.11 = (bf16[1,128,512]{2,1,0:T(8,128)(2,1)S(1)}, bf16[1,128,512]{2,1,0:T(8,128)(2,1)S(1)}, u32[]{:S(2)}, u32[]{:S(2)}) collective-permute-start(bf16[1,128,512]{2,1,0:T(8,128)(2,1)S(1)} %get-tuple-element.8), channel_id=1, source_target_pairs={{2,0},{3,1},{6,4},{7,5},{10,8},{11,9},{14,12},{15,13},{18,16},{19,... | collective-permute-start | bytes 393224 | tf_op jit(solution)/shard_map/ppermute | solution.py:22
  132.4 8.2 %collective-permute-start.8 = (bf16[1,128,512]{2,1,0:T(8,128)(2,1)S(1)}, bf16[1,128,512]{2,1,0:T(8,128)(2,1)S(1)}, u32[]{:S(2)}, u32[]{:S(2)}) collective-permute-start(bf16[1,128,512]{2,1,0:T(8,128)(2,1)S(1)} %get-tuple-element.7), channel_id=1, source_target_pairs={{0,4},{4,8},{8,12},{12,0},{1,5},{5,9},{9,13},{13,1},{2,6},{6,10},{... | collective-permute-start | bytes 393224 | tf_op jit(solution)/shard_map/ppermute | solution.py:19
  134.0 8.0 %collective-permute-start.9 = (bf16[1,128,512]{2,1,0:T(8,128)(2,1)S(1)}, bf16[1,128,512]{2,1,0:T(8,128)(2,1)S(1)}, u32[]{:S(2)}, u32[]{:S(2)}) collective-permute-start(bf16[1,128,512]{2,1,0:T(8,128)(2,1)S(1)} %get-tuple-element.10), channel_id=1, source_target_pairs={{4,0},{8,4},{12,8},{0,12},{5,1},{9,5},{13,9},{1,13},{6,2},{10,6},{... | collective-permute-start | bytes 393224 | tf_op jit(solution)/shard_map/ppermute | solution.py:22
  143.8 47.1 %all-reduce.3.cloned.1.call-start = ((), (), s32[]{:S(2)}) async-start(), calls=%async_computation.6 | async-start | bytes 524288 | tf_op jit(solution)/shard_map/psum | solution.py:8
  171.8 45.7 %all-reduce.5.cloned.1.call-start = ((), (), s32[]{:S(2)}) async-start(), calls=%async_computation.7 | async-start | bytes 524288 | tf_op jit(solution)/shard_map/psum | solution.py:8
  (16 other events, 74.4 us)
Sparse Core Ops, SparseCore 0:
  50.3 7.6 reduce-scatter.3
  101.9 7.3 reduce-scatter.5
  143.9 27.7 reduce-scatter.7
  174.0 16.8 all-reduce.2
  193.1 24.3 all-reduce.4
